TPU v7x, 512 devices: a whole 4x4x16 slice. The times are simulated.
512 devices in a mesh: freq: 32 (over z_lo, x), src: 2 (over z_hi), rcv: 8 (over y, core).
Axes of the slice: x: 4, y: 4, z: 16 (z_hi: 2, z_lo: 8; z = z_hi * 8 + z_lo), core: 2. Of those that a mesh axis runs over, the one named last changes fastest.
Arguments:
- traces: float32 [1024, 1024, 256], P(('src', 'freq'), 'rcv'), may hold values from -6 to 6
Outputs:
- multiples: float32 [2, 96, 1024, 1024], P(None, 'freq', 'src', 'rcv')
All inputs are finite; a program needn't handle non-finite values.
Results may differ from a plain program's by a relative error of at most 0.000098.
Values sent between devices are 32-bit elements; how exact they have to be, the bound alone decides.
A program may use at most 64 MiB of HBM per device.

v0:
```python
import math
import jax
import jax.numpy as jnp
from jax import lax
from jax.sharding import PartitionSpec as P

N = 1024
FPD = 3


def dft_matrix(n_time, n_freq):
    times = jnp.arange(n_time, dtype=jnp.int32)
    bins = jnp.arange(n_freq, dtype=jnp.int32)
    phase = times[:, None] * bins[None, :] % n_time
    angle = phase.astype(jnp.float32) * (2.0 * math.pi / n_time)
    both = jnp.stack([jnp.cos(angle), -jnp.sin(angle)], axis=-1)
    return both.reshape(n_time, 2 * n_freq) * (1.0 / math.sqrt(n_time))


def batched_dot(left, right):
    return jnp.einsum(
        "mgq,mqn->mgn",
        left,
        right,
        precision=lax.Precision.HIGHEST,
        preferred_element_type=jnp.float32,
    )


def complex_product(left_re, left_im, right_re, right_im):
    real_part = batched_dot(left_re, right_re) - batched_dot(left_im, right_im)
    imag_part = batched_dot(left_re, right_im) + batched_dot(left_im, right_re)
    return (real_part, imag_part)


def per_device(traces):
    n_time = traces.shape[2]
    n_freq = FPD * lax.axis_size("freq")
    dft_table = dft_matrix(n_time, n_freq)
    spectra = jnp.einsum(
        "srt,tk->ksr",
        traces,
        dft_table,
        precision=lax.Precision.HIGHEST,
        preferred_element_type=jnp.float32,
    )
    regrouped = lax.all_to_all(spectra, "freq", split_axis=0, concat_axis=1, tiled=True)
    src_rows = regrouped.shape[1]
    rcv_cols = regrouped.shape[2]
    split_parts = regrouped.reshape(FPD, 2, src_rows, rcv_cols)
    local_re = split_parts[:, 0]
    local_im = split_parts[:, 1]
    col_re, col_im = (
        lax.all_gather(local_re, "src", axis=1, tiled=True),
        lax.all_gather(local_im, "src", axis=1, tiled=True),
    )
    piece_re = lax.all_gather(local_re, "rcv", axis=2, tiled=True)
    piece_im = lax.all_gather(local_im, "rcv", axis=2, tiled=True)
    real_part, imag_part = complex_product(piece_re, piece_im, col_re, col_im)
    scale = -1.0 / math.sqrt(N)
    return jnp.stack([real_part, imag_part]) * scale


def solution(mesh):
    in_specs = (P(("src", "freq"), "rcv", None),)
    out_specs = P(None, "freq", "src", "rcv")
    return jax.shard_map(
        per_device, mesh=mesh, in_specs=in_specs, out_specs=out_specs, check_vma=False
    )
```

profile of v0, /device:TPU:1, one launch (start us, length us, event | category | flops | bytes accessed | tf_op | source)
XLA Modules:
  0.0 411.7 jit_solution(3908307167513742405)
XLA Ops:
  6.5 0.0 copy-start
  6.5 0.0 all-gather.11.cloned.1.call-start
  6.5 0.4 sine_negate_fusion
  7.0 0.2 copy.14
  7.1 0.1 reshape.83
  7.3 0.8 copy-done
  8.1 2.3 fusion.39
  10.4 0.9 copy.15
  11.3 89.4 %all_to_all.15 = f32[192,16,128]{2,1,0:T(8,128)S(1)} all-to-all(f32[192,16,128]{2,1,0:T(8,128)S(1)} %copy.15), channel_id=1, replica_groups=mesh['freq'=32,'src'=2,'rcv'=8] {'freq'}, dimensions={0} | all-to-all | bytes 3145728 | tf_op jit(solution)/shard_map/all_to_all | solution.py:47
  100.7 0.1 copy.16
  100.9 1.3 slice_bitcast_fusion.1
  102.1 0.0 all-gather.11.cloned.1.call-update
  102.1 0.0 all-gather.13.cloned.1.call-start
  102.2 0.7 all-gather.13.cloned.1.call-update
  102.9 0.0 all-gather.15.cloned.1.call-start
  102.9 0.7 all-gather.15.cloned.1.call-update
  103.6 0.2 all-gather.9.cloned.1.call-start
  103.9 0.3 all-gather.9.cloned.1.call-update
  104.2 90.4 %all-gather.11.cloned.1.call-done = f32[3,1,1024,128]{3,2,0,1:T(8,128)} async-done(((f32[3,1,512,128]{3,2,0,1:T(8,128)}), f32[3,1,1024,128]{3,2,0,1:T(8,128)}) %all-gather.11.cloned.1.call-update) | async-done | bytes 1572880 | tf_op jit(solution)/shard_map/all_gather | solution.py:54
  194.6 48.8 %all-gather.13.cloned.1.call-done = f32[3,1,512,1024]{3,2,0,1:T(8,128)} async-done(((f32[3,1,512,128]{3,2,0,1:T(8,128)}), f32[3,1,512,1024]{3,2,0,1:T(8,128)}) %all-gather.13.cloned.1.call-update) | async-done | bytes 6291472 | tf_op jit(solution)/shard_map/all_gather | solution.py:58
  243.4 7.9 %fusion = f32[3,512,128]{2,1,0:T(8,128)S(1)} fusion(f32[3,1,512,1024]{3,2,0,1:T(8,128)} %all-gather.13.cloned.1.call-done, f32[3,1,1024,128]{3,2,0,1:T(8,128)} %all-gather.11.cloned.1.call-done), kind=kOutput, calls=%fused_computation | convolution fusion | flops 2415919104 | bytes 8650752 | tf_op jit(solution)/shard_map/mgq,mqn->mgn/dot_general | solution.py:21
  251.3 90.1 %all-gather.15.cloned.1.call-done = f32[3,1,1024,128]{3,2,0,1:T(8,128)} async-done(((f32[3,1,512,128]{3,2,0,1:T(8,128)}), f32[3,1,1024,128]{3,2,0,1:T(8,128)}) %all-gather.15.cloned.1.call-update) | async-done | bytes 1572880 | tf_op jit(solution)/shard_map/all_gather | solution.py:55
  341.4 8.8 %fusion.2 = f32[3,512,128]{2,1,0:T(8,128)} fusion(f32[3,1,512,1024]{3,2,0,1:T(8,128)} %all-gather.13.cloned.1.call-done, f32[3,1,1024,128]{3,2,0,1:T(8,128)} %all-gather.15.cloned.1.call-done), kind=kOutput, calls=%fused_computation.2 | convolution fusion | flops 2415919104 | bytes 8650752 | tf_op jit(solution)/shard_map/mgq,mqn->mgn/dot_general | solution.py:21
  350.2 39.8 %all-gather.9.cloned.1.call-done = f32[3,1,512,1024]{3,2,0,1:T(8,128)} async-done(((f32[3,1,512,128]{3,2,0,1:T(8,128)}), f32[3,1,512,1024]{3,2,0,1:T(8,128)}) %all-gather.9.cloned.1.call-update) | async-done | bytes 6291472 | tf_op jit(solution)/shard_map/all_gather | solution.py:57
  390.1 0.0 copy-start.1
  390.1 0.0 copy-start.2
  390.1 0.0 copy-start.3
  390.1 8.4 %fusion.22 = f32[1,3,512,128]{3,2,1,0:T(8,128)S(1)} fusion(f32[3,512,128]{2,1,0:T(8,128)S(1)} %fusion, f32[3,1,1024,128]{3,2,0,1:T(8,128)} %all-gather.15.cloned.1.call-done, f32[3,1,512,1024]{3,2,0,1:T(8,128)} %all-gather.9.cloned.1.call-done), kind=kOutput, calls=%fused_computation.15 | convolution fusion | flops 2416115712 | bytes 9437184 | tf_op jit(solution)/shard_map/mgq,mqn->mgn/dot_general | solution.py:21
  398.5 0.0 copy-done.1
  398.5 0.0 copy-done.2
  398.5 0.0 copy-done.3
  398.5 5.4 %fusion.27 = f32[1,3,512,128]{3,2,1,0:T(8,128)S(1)} fusion(f32[3,512,128]{2,1,0:T(8,128)S(1)} %copy-done.3, f32[3,1,1024,128]{3,2,0,1:T(8,128)S(1)} %copy-done.2, f32[3,1,512,1024]{3,2,0,1:T(8,128)S(1)} %copy-done.1), kind=kOutput, calls=%fused_computation.16 | convolution fusion | flops 2416115712 | bytes 9437184 | tf_op jit(solution)/shard_map/mgq,mqn->mgn/dot_general | solution.py:21
  403.9 1.2 maximum_multiply_fusion
  (1 shorter events, 0.0 us)
Async XLA Ops:
  6.5 1.6 copy-start
  6.5 188.0 %all-gather.11.cloned.1.call-start = ((), (), s32[]{:S(2)}) async-start(), calls=%async_computation.2 | async-start | bytes 2359296 | tf_op jit(solution)/shard_map/all_gather | solution.py:54
  102.1 141.2 %all-gather.13.cloned.1.call-start = ((), (), s32[]{:S(2)}) async-start(), calls=%async_computation.3 | async-start | bytes 7077888 | tf_op jit(solution)/shard_map/all_gather | solution.py:58
  102.9 238.5 %all-gather.15.cloned.1.call-start = ((), (), s32[]{:S(2)}) async-start(), calls=%async_computation.4 | async-start | bytes 2359296 | tf_op jit(solution)/shard_map/all_gather | solution.py:55
  103.6 286.5 %all-gather.9.cloned.1.call-start = ((), (), s32[]{:S(2)}) async-start(), calls=%async_computation.1 | async-start | bytes 7077888 | tf_op jit(solution)/shard_map/all_gather | solution.py:57
  390.1 8.4 %copy-start.1 = (f32[3,1,512,1024]{3,2,0,1:T(8,128)S(1)}, f32[3,1,512,1024]{3,2,0,1:T(8,128)}, u32[]{:S(2)}) copy-start(f32[3,1,512,1024]{3,2,0,1:T(8,128)} %all-gather.9.cloned.1.call-done) | copy-start | bytes 18874372
  390.1 8.4 %copy-start.2 = (f32[3,1,1024,128]{3,2,0,1:T(8,128)S(1)}, f32[3,1,1024,128]{3,2,0,1:T(8,128)}, u32[]{:S(2)}) copy-start(f32[3,1,1024,128]{3,2,0,1:T(8,128)} %all-gather.11.cloned.1.call-done) | copy-start | bytes 4718596
  390.1 8.4 %copy-start.3 = (f32[3,512,128]{2,1,0:T(8,128)S(1)}, f32[3,512,128]{2,1,0:T(8,128)}, u32[]{:S(2)}) copy-start(f32[3,512,128]{2,1,0:T(8,128)} %fusion.2) | copy-start | bytes 2359300
Sparse Core Ops, SparseCore 0:
  102.3 92.2 all-gather.10
  196.7 46.6 all-gather.12
  245.5 95.8 all-gather.14
  343.4 46.6 all-gather.8
where the time goes:
time: 412 us
  waiting for transfers between devices  271 us (66%)
  blocking collectives  89.4 us (22%)
  matrix products  32.8 us (8%)
  between operations  13.2 us (3%)
    all_gather x1, waiting for transfers between devices, per_device(): lax.all_gather(local_re, 'src', axis=1, tiled=True)  90.4 us
    all_gather x1, waiting for transfers between devices, per_device(): lax.all_gather(local_im, 'src', axis=1, tiled=True)  90.1 us
    all_to_all x1, blocking collectives, per_device(): lax.all_to_all(spectra, 'freq', split_axis=0, concat_axis=1, tiled=True)  89.4 us
    all_gather x1, waiting for transfers between devices, per_device(): piece_im = lax.all_gather(local_im, 'rcv', axis=2, tiled=True)  48.8 us
    all_gather x1, waiting for transfers between devices, per_device(): piece_re = lax.all_gather(local_re, 'rcv', axis=2, tiled=True)  39.8 us
    dot_general x4, matrix products, batched_dot(): jnp.einsum('mgq,mqn->mgn', left, right, precision=lax.Precision.HIGHEST,...  30.5 us
  transfers between devices with their start and end apart: 4, of which 4 were waited for; matrix products, arithmetic and copies ran while one was open for 4% of the time, Pallas kernels for 0%

commit v1 on v0

--- a/solution.py
+++ b/solution.py
@@ -44,7 +44,10 @@
         precision=lax.Precision.HIGHEST,
         preferred_element_type=jnp.float32,
     )
-    regrouped = lax.all_to_all(spectra, "freq", split_axis=0, concat_axis=1, tiled=True)
+    regrouped = jnp.concatenate(
+        lax.all_to_all(jnp.stack(jnp.split(spectra, lax.axis_size("freq"), axis=0)), "freq", 0, 0),
+        axis=1,
+    )
     src_rows = regrouped.shape[1]
     rcv_cols = regrouped.shape[2]
     split_parts = regrouped.reshape(FPD, 2, src_rows, rcv_cols)

time: 412 us -> 412 us (level)
  no operation moved by 1% of the time
where the time goes in v1:
time: 412 us
  waiting for transfers between devices  271 us (66%)
  blocking collectives  89.4 us (22%)
  matrix products  32.8 us (8%)
  between operations  13.5 us (3%)
    all_gather x1, waiting for transfers between devices, per_device(): lax.all_gather(local_re, 'src', axis=1, tiled=True)  90.4 us
    all_gather x1, waiting for transfers between devices, per_device(): lax.all_gather(local_im, 'src', axis=1, tiled=True)  90.1 us
    all_to_all x1, blocking collectives, per_device(): lax.all_to_all(jnp.stack(jnp.split(spectra, lax.axis_size('freq'), axis=0...  89.4 us
    all_gather x1, waiting for transfers between devices, per_device(): piece_im = lax.all_gather(local_im, 'rcv', axis=2, tiled=True)  48.8 us
    all_gather x1, waiting for transfers between devices, per_device(): piece_re = lax.all_gather(local_re, 'rcv', axis=2, tiled=True)  39.8 us
    dot_general x4, matrix products, batched_dot(): jnp.einsum('mgq,mqn->mgn', left, right, precision=lax.Precision.HIGHEST,...  30.5 us
  transfers between devices with their start and end apart: 4, of which 4 were waited for; matrix products, arithmetic and copies ran while one was open for 4% of the time, Pallas kernels for 0%

profile of v1, /device:TPU:1, one launch (start us, length us, event | category | flops | bytes accessed | tf_op | source)
XLA Modules:
  0.0 411.7 jit_solution(864384014348216134)
XLA Ops:
  6.5 0.0 copy-start
  6.5 0.0 all-gather.11.cloned.1.call-start
  6.5 0.4 sine_negate_fusion
  7.0 0.2 copy.15
  7.1 0.1 reshape.82
  7.3 0.8 copy-done
  8.1 2.3 fusion.39
  11.1 0.3 copy.16
  11.4 89.4 %all_to_all.5 = f32[32,6,16,128]{3,2,1,0:T(8,128)S(1)} all-to-all(f32[32,6,16,128]{3,2,1,0:T(8,128)S(1)} %copy.16), channel_id=1, replica_groups=mesh['freq'=32,'src'=2,'rcv'=8] {'freq'}, dimensions={0} | all-to-all | bytes 3145728 | tf_op jit(solution)/shard_map/all_to_all | solution.py:48
  100.7 0.1 copy.17
  100.9 1.3 slice_bitcast_fusion.1
  102.1 0.0 all-gather.11.cloned.1.call-update
  102.1 0.0 all-gather.13.cloned.1.call-start
  102.2 0.7 all-gather.13.cloned.1.call-update
  102.9 0.0 all-gather.15.cloned.1.call-start
  102.9 0.7 all-gather.15.cloned.1.call-update
  103.6 0.2 all-gather.9.cloned.1.call-start
  103.9 0.3 all-gather.9.cloned.1.call-update
  104.2 90.4 %all-gather.11.cloned.1.call-done = f32[3,1,1024,128]{3,2,0,1:T(8,128)} async-done(((f32[3,1,512,128]{3,2,0,1:T(8,128)}), f32[3,1,1024,128]{3,2,0,1:T(8,128)}) %all-gather.11.cloned.1.call-update) | async-done | bytes 1572880 | tf_op jit(solution)/shard_map/all_gather | solution.py:57
  194.6 48.8 %all-gather.13.cloned.1.call-done = f32[3,1,512,1024]{3,2,0,1:T(8,128)} async-done(((f32[3,1,512,128]{3,2,0,1:T(8,128)}), f32[3,1,512,1024]{3,2,0,1:T(8,128)}) %all-gather.13.cloned.1.call-update) | async-done | bytes 6291472 | tf_op jit(solution)/shard_map/all_gather | solution.py:61
  243.4 7.9 %fusion = f32[3,512,128]{2,1,0:T(8,128)S(1)} fusion(f32[3,1,512,1024]{3,2,0,1:T(8,128)} %all-gather.13.cloned.1.call-done, f32[3,1,1024,128]{3,2,0,1:T(8,128)} %all-gather.11.cloned.1.call-done), kind=kOutput, calls=%fused_computation | convolution fusion | flops 2415919104 | bytes 8650752 | tf_op jit(solution)/shard_map/mgq,mqn->mgn/dot_general | solution.py:21
  251.4 90.1 %all-gather.15.cloned.1.call-done = f32[3,1,1024,128]{3,2,0,1:T(8,128)} async-done(((f32[3,1,512,128]{3,2,0,1:T(8,128)}), f32[3,1,1024,128]{3,2,0,1:T(8,128)}) %all-gather.15.cloned.1.call-update) | async-done | bytes 1572880 | tf_op jit(solution)/shard_map/all_gather | solution.py:58
  341.4 8.8 %fusion.2 = f32[3,512,128]{2,1,0:T(8,128)} fusion(f32[3,1,512,1024]{3,2,0,1:T(8,128)} %all-gather.13.cloned.1.call-done, f32[3,1,1024,128]{3,2,0,1:T(8,128)} %all-gather.15.cloned.1.call-done), kind=kOutput, calls=%fused_computation.2 | convolution fusion | flops 2415919104 | bytes 8650752 | tf_op jit(solution)/shard_map/mgq,mqn->mgn/dot_general | solution.py:21
  350.2 39.8 %all-gather.9.cloned.1.call-done = f32[3,1,512,1024]{3,2,0,1:T(8,128)} async-done(((f32[3,1,512,128]{3,2,0,1:T(8,128)}), f32[3,1,512,1024]{3,2,0,1:T(8,128)}) %all-gather.9.cloned.1.call-update) | async-done | bytes 6291472 | tf_op jit(solution)/shard_map/all_gather | solution.py:60
  390.1 0.0 copy-start.1
  390.1 0.0 copy-start.2
  390.1 0.0 copy-start.3
  390.1 8.4 %fusion.22 = f32[1,3,512,128]{3,2,1,0:T(8,128)S(1)} fusion(f32[3,512,128]{2,1,0:T(8,128)S(1)} %fusion, f32[3,1,1024,128]{3,2,0,1:T(8,128)} %all-gather.15.cloned.1.call-done, f32[3,1,512,1024]{3,2,0,1:T(8,128)} %all-gather.9.cloned.1.call-done), kind=kOutput, calls=%fused_computation.15 | convolution fusion | flops 2416115712 | bytes 9437184 | tf_op jit(solution)/shard_map/mgq,mqn->mgn/dot_general | solution.py:21
  398.5 0.0 copy-done.1
  398.5 0.0 copy-done.2
  398.5 0.0 copy-done.3
  398.5 5.4 %fusion.27 = f32[1,3,512,128]{3,2,1,0:T(8,128)S(1)} fusion(f32[3,512,128]{2,1,0:T(8,128)S(1)} %copy-done.3, f32[3,1,1024,128]{3,2,0,1:T(8,128)S(1)} %copy-done.2, f32[3,1,512,1024]{3,2,0,1:T(8,128)S(1)} %copy-done.1), kind=kOutput, calls=%fused_computation.16 | convolution fusion | flops 2416115712 | bytes 9437184 | tf_op jit(solution)/shard_map/mgq,mqn->mgn/dot_general | solution.py:21
  403.9 1.2 maximum_multiply_fusion
  (33 shorter events, 0.4 us)
Async XLA Ops:
  6.5 1.6 copy-start
  6.5 188.0 %all-gather.11.cloned.1.call-start = ((), (), s32[]{:S(2)}) async-start(), calls=%async_computation.2 | async-start | bytes 2359296 | tf_op jit(solution)/shard_map/all_gather | solution.py:57
  102.1 141.2 %all-gather.13.cloned.1.call-start = ((), (), s32[]{:S(2)}) async-start(), calls=%async_computation.3 | async-start | bytes 7077888 | tf_op jit(solution)/shard_map/all_gather | solution.py:61
  102.9 238.5 %all-gather.15.cloned.1.call-start = ((), (), s32[]{:S(2)}) async-start(), calls=%async_computation.4 | async-start | bytes 2359296 | tf_op jit(solution)/shard_map/all_gather | solution.py:58
  103.6 286.5 %all-gather.9.cloned.1.call-start = ((), (), s32[]{:S(2)}) async-start(), calls=%async_computation.1 | async-start | bytes 7077888 | tf_op jit(solution)/shard_map/all_gather | solution.py:60
  390.1 8.4 %copy-start.1 = (f32[3,1,512,1024]{3,2,0,1:T(8,128)S(1)}, f32[3,1,512,1024]{3,2,0,1:T(8,128)}, u32[]{:S(2)}) copy-start(f32[3,1,512,1024]{3,2,0,1:T(8,128)} %all-gather.9.cloned.1.call-done) | copy-start | bytes 18874372
  390.1 8.4 %copy-start.2 = (f32[3,1,1024,128]{3,2,0,1:T(8,128)S(1)}, f32[3,1,1024,128]{3,2,0,1:T(8,128)}, u32[]{:S(2)}) copy-start(f32[3,1,1024,128]{3,2,0,1:T(8,128)} %all-gather.11.cloned.1.call-done) | copy-start | bytes 4718596
  390.1 8.4 %copy-start.3 = (f32[3,512,128]{2,1,0:T(8,128)S(1)}, f32[3,512,128]{2,1,0:T(8,128)}, u32[]{:S(2)}) copy-start(f32[3,512,128]{2,1,0:T(8,128)} %fusion.2) | copy-start | bytes 2359300
Sparse Core Ops, SparseCore 0:
  102.3 92.2 all-gather.10
  196.7 46.6 all-gather.12
  245.5 95.8 all-gather.14
  343.4 46.6 all-gather.8
